TPU v7x, 256 devices: a whole 4x4x8 slice. The times are simulated.
256 devices in a mesh: row: 32 (over x_hi, z, core), col: 8 (over x_lo, y).
Axes of the slice: x: 4 (x_hi: 2, x_lo: 2; x = x_hi * 2 + x_lo), y: 4, z: 8, core: 2. Of those that a mesh axis runs over, the one named last changes fastest.
Arguments:
- eigvecs: float32 [8192, 8192], P('row', 'col'), may hold values from -6 to 6
- panels: float32 [5, 32, 256, 128], P(None, 'row', 'col'), may hold values from -6 to 6
- sweep_shift: int32 [5], replicated, may hold values from 0 to 31
- slot_group: int32 [5, 32], replicated, may hold values from 0 to 31, each once within a row
Outputs:
- full_vectors: float32 [8192, 8192], P('row', 'col')
Inputs may be any that keep to these rules, and one draw needn't show every extreme that they name: Each row of slot_group names each of the 32 groups once.
All inputs are finite; a program needn't handle non-finite values.
Results may differ from a plain program's by a relative error of at most 0.00029.
Values sent between devices are 32-bit elements; how exact they have to be, the bound alone decides.
A program may use at most 128 MiB of HBM per device.

v0:
```python
import jax
import jax.numpy as jnp
from jax import lax
from jax.sharding import PartitionSpec as P

SWEEPS = 5


PRECISE = lax.Precision.HIGHEST


def passed_along(block, axis, distance):
    devices = range(lax.axis_size(axis))
    route = [((i - distance) % len(devices), i) for i in devices]
    return lax.ppermute(block, axis, route)


def invert_upper(factor):
    groups, order_now, _ = factor.shape
    diagonal_vals = jnp.sum(factor * jnp.eye(order_now, dtype=factor.dtype), axis=2)
    blocks = (1.0 / diagonal_vals).reshape(groups, order_now, 1, 1)
    width_now = 1
    while width_now < order_now:
        halves = order_now // (2 * width_now)
        grouped = factor.reshape(groups, halves, 2 * width_now, halves, 2 * width_now)
        picker = jnp.eye(halves, dtype=factor.dtype)
        paired = jnp.einsum("gpaqb,pq->gpab", grouped, picker, precision=PRECISE)
        upper_right = paired[:, :, :width_now, width_now:]
        pairs = blocks.reshape(groups, halves, 2, width_now, width_now)
        first_inv = pairs[:, :, 0]
        second = pairs[:, :, 1]
        inner = jnp.einsum("gpab,gpbc->gpac", upper_right, second, precision=PRECISE)
        corner = -jnp.einsum("gpab,gpbc->gpac", first_inv, inner, precision=PRECISE)
        zero_block = jnp.zeros_like(corner)
        top_rows = jnp.concatenate([first_inv, corner], axis=3)
        bottom = jnp.concatenate([zero_block, second], axis=3)
        blocks = jnp.concatenate([top_rows, bottom], axis=2)
        width_now = width_now * 2
    return blocks.reshape(groups, order_now, order_now)


def apply_groups(vectors, windows):
    products = jnp.einsum("gwb,gwc->gbc", vectors, vectors, precision=PRECISE)
    ident = jnp.eye(products.shape[1], dtype=products.dtype)
    factor = jnp.triu(products, 1) + 0.5 * products * ident
    inverse = invert_upper(factor)
    projected = jnp.einsum("gwb,gwc->gbc", vectors, windows, precision=PRECISE)
    coeffs = jnp.einsum("gab,gbc->gac", inverse, projected, precision=PRECISE)
    return windows - jnp.einsum("gwb,gbc->gwc", vectors, coeffs, precision=PRECISE)


def on_device(eigvecs, panels, sweep_shift, slot_group):
    rows_dev, cols_dev = eigvecs.shape
    band_width = panels.shape[3]
    window_rows = 2 * band_width
    local_groups = rows_dev // window_rows
    row_count = lax.axis_size("row")
    total_groups = local_groups * row_count
    rank_here = lax.axis_index("row")
    positions = rank_here * local_groups + jnp.arange(local_groups, dtype=jnp.int32)
    for sweep_step in range(SWEEPS):
        rotation = sweep_shift[sweep_step]
        slot_owner = slot_group[sweep_step]
        stored = panels[sweep_step]
        gathered = lax.all_gather(stored, "row", axis=0, tiled=True)
        wanted = (positions - rotation) % total_groups
        selector = (wanted[:, None] == slot_owner[None, :]).astype(jnp.float32)
        my_panel = jnp.einsum("gs,swb->gwb", selector, gathered, precision=PRECISE)
        reflect = lax.all_gather(my_panel, "col", axis=1, tiled=True)
        if sweep_step % 2 == 0:
            windows = eigvecs.reshape(local_groups, window_rows, cols_dev)
            eigvecs = apply_groups(reflect, windows).reshape(rows_dev, cols_dev)
        else:
            following = passed_along(eigvecs[:band_width], "row", -1)
            joined = jnp.concatenate([eigvecs[band_width:], following], axis=0)
            result = apply_groups(reflect, joined.reshape(local_groups, window_rows, cols_dev))
            result = result.reshape(rows_dev, cols_dev)
            returned = passed_along(result[rows_dev - band_width :], "row", 1)
            eigvecs = jnp.concatenate([returned, result[: rows_dev - band_width]], axis=0)
    return eigvecs


def solution(mesh):
    in_specs = (P("row", "col"), P(None, "row", "col", None), P(), P())
    out_specs = P("row", "col")
    return jax.shard_map(
        on_device, mesh=mesh, in_specs=in_specs, out_specs=out_specs, check_vma=False
    )
```

profile of v0, /device:TPU:24, one launch (start us, length us, event | category | flops | bytes accessed | tf_op | source)
XLA Modules:
  0.0 626.6 jit_solution(11593037996810764836)
XLA Ops:
  1.7 1.5 fusion.358
  3.8 1.4 fusion.352
  5.3 46.1 %all-gather = f32[32,1,32,128]{3,2,1,0:T(8,128)S(1)} all-gather(f32[1,1,32,128]{3,2,1,0:T(8,128)S(1)} %get-tuple-element.33), channel_id=2, replica_groups=mesh['row'=32,'col'=8] {'row'}, dimensions={0}, use_global_device_ids=true | all-gather | bytes 540672 | tf_op jit(solution)/shard_map/all_gather | solution.py:65
  52.6 28.2 %all-gather.1 = f32[256,128]{1,0:T(8,128)S(1)} all-gather(f32[32,128]{1,0:T(8,128)S(1)} %bitcast.1029), channel_id=3, replica_groups=mesh['row'=32,'col'=8] {'col'}, dimensions={0}, use_global_device_ids=true | all-gather | bytes 147456 | tf_op jit(solution)/shard_map/all_gather | solution.py:69
  80.8 1.6 fusion.347
  82.5 5.7 reshape.1202
  88.2 2.1 reshape.1207
  93.6 4.3 fusion.51
  97.8 1.6 copy.288
  104.2 1.4 reshape.1205
  105.6 2.2 slice_reduce_fusion.19
  107.8 1.9 copy.347
  109.7 1.4 fusion.101
  127.9 41.9 %all-gather.8 = f32[32,1,32,128]{3,2,1,0:T(8,128)S(1)} all-gather(f32[1,1,32,128]{3,2,1,0:T(8,128)S(1)} %copy-done.26), channel_id=10, replica_groups=mesh['row'=32,'col'=8] {'row'}, dimensions={0}, use_global_device_ids=true | all-gather | bytes 540672 | tf_op jit(solution)/shard_map/all_gather | solution.py:65
  170.3 28.2 %all-gather.9 = f32[256,128]{1,0:T(8,128)S(1)} all-gather(f32[32,128]{1,0:T(8,128)S(1)} %bitcast.1030), channel_id=11, replica_groups=mesh['row'=32,'col'=8] {'col'}, dimensions={0}, use_global_device_ids=true | all-gather | bytes 147456 | tf_op jit(solution)/shard_map/all_gather | solution.py:69
  198.6 1.6 fusion.351
  200.3 5.5 reshape.1346
  205.8 3.5 reshape.1351
  209.2 1.6 reshape.1356
  213.5 37.8 %all-gather.6 = f32[32,1,32,128]{3,2,1,0:T(8,128)S(1)} all-gather(f32[1,1,32,128]{3,2,1,0:T(8,128)S(1)} %copy-done.25), channel_id=8, replica_groups=mesh['row'=32,'col'=8] {'row'}, dimensions={0}, use_global_device_ids=true | all-gather | bytes 540672 | tf_op jit(solution)/shard_map/all_gather | solution.py:65
  251.9 28.2 %all-gather.7 = f32[256,128]{1,0:T(8,128)S(1)} all-gather(f32[32,128]{1,0:T(8,128)S(1)} %bitcast.1031), channel_id=9, replica_groups=mesh['row'=32,'col'=8] {'col'}, dimensions={0}, use_global_device_ids=true | all-gather | bytes 147456 | tf_op jit(solution)/shard_map/all_gather | solution.py:69
  280.1 1.5 fusion.350
  281.8 5.5 reshape.1310
  287.3 3.5 reshape.1315
  290.8 1.6 reshape.1320
  296.3 39.8 %all-gather.4 = f32[32,1,32,128]{3,2,1,0:T(8,128)S(1)} all-gather(f32[1,1,32,128]{3,2,1,0:T(8,128)S(1)} %copy-done.24), channel_id=6, replica_groups=mesh['row'=32,'col'=8] {'row'}, dimensions={0}, use_global_device_ids=true | all-gather | bytes 540672 | tf_op jit(solution)/shard_map/all_gather | solution.py:65
  336.7 28.2 %all-gather.5 = f32[256,128]{1,0:T(8,128)S(1)} all-gather(f32[32,128]{1,0:T(8,128)S(1)} %bitcast.1032), channel_id=7, replica_groups=mesh['row'=32,'col'=8] {'col'}, dimensions={0}, use_global_device_ids=true | all-gather | bytes 147456 | tf_op jit(solution)/shard_map/all_gather | solution.py:69
  364.9 1.6 fusion.349
  366.6 5.5 reshape.1274
  372.1 3.5 reshape.1279
  375.6 1.6 reshape.1284
  379.9 37.8 %all-gather.2 = f32[32,1,32,128]{3,2,1,0:T(8,128)S(1)} all-gather(f32[1,1,32,128]{3,2,1,0:T(8,128)S(1)} %copy-done.23), channel_id=4, replica_groups=mesh['row'=32,'col'=8] {'row'}, dimensions={0}, use_global_device_ids=true | all-gather | bytes 540672 | tf_op jit(solution)/shard_map/all_gather | solution.py:65
  418.3 28.2 %all-gather.3 = f32[256,128]{1,0:T(8,128)S(1)} all-gather(f32[32,128]{1,0:T(8,128)S(1)} %bitcast.1033), channel_id=5, replica_groups=mesh['row'=32,'col'=8] {'col'}, dimensions={0}, use_global_device_ids=true | all-gather | bytes 147456 | tf_op jit(solution)/shard_map/all_gather | solution.py:69
  446.5 1.6 fusion.348
  448.1 5.7 reshape.1238
  453.8 2.1 reshape.1243
  456.0 1.6 reshape.1248
  459.5 3.7 fusion.45
  464.4 3.7 fusion.43
  474.4 2.4 fusion.93
  480.0 1.7 fusion.254
  483.5 2.1 copy.340
  485.6 1.4 fusion.265
  489.0 1.8 copy.342
  494.0 1.7 copy.344
  500.8 2.4 fusion.95
  508.2 1.7 fusion.256
  512.3 2.0 copy.329
  517.8 1.8 copy.331
  522.8 1.7 copy.333
  528.2 3.7 fusion.49
  533.1 3.7 fusion.47
  540.7 2.4 fusion.97
  546.3 1.7 fusion.258
  550.4 2.0 copy.318
  556.5 1.8 copy.320
  561.5 1.7 copy.322
  572.9 1.7 fusion.260
  581.9 1.8 fusion.32
  584.3 2.0 fusion.2
  587.0 11.8 %collective-permute-done.1 = f32[128,1024]{1,0:T(8,128)S(1)} collective-permute-done((f32[128,1024]{1,0:T(8,128)S(1)}, f32[128,1024]{1,0:T(8,128)S(1)}, u32[]{:S(2)}, u32[]{:S(2)}) %collective-permute-start.1) | collective-permute-done | bytes 524320 | tf_op jit(solution)/shard_map/ppermute | solution.py:15
  601.9 6.3 collective-permute-done.2
  611.2 11.9 %collective-permute-done.3 = f32[128,1024]{1,0:T(8,128)S(1)} collective-permute-done((f32[128,1024]{1,0:T(8,128)S(1)}, f32[128,1024]{1,0:T(8,128)S(1)}, u32[]{:S(2)}, u32[]{:S(2)}) %collective-permute-start.3) | collective-permute-done | bytes 524320 | tf_op jit(solution)/shard_map/ppermute | solution.py:15
  624.5 1.9 convolution_subtract_fusion
  (319 shorter events, 122.3 us)
Async XLA Ops:
  97.8 22.3 %copy-start.1 = (f32[4,32,4,32]{1,0,3,2:T(4,128)S(1)}, f32[4,32,4,32]{1,0,3,2:T(4,128)}, u32[]{:S(2)}) copy-start(f32[4,32,4,32]{1,0,3,2:T(4,128)} %reshape.1222) | copy-start | bytes 196612
  111.2 10.6 %copy-start.2 = (f32[2,64,2,64]{1,0,3,2:T(2,128)S(1)}, f32[2,64,2,64]{1,0,3,2:T(2,128)}, u32[]{:S(2)}) copy-start(f32[2,64,2,64]{1,0,3,2:T(2,128)} %reshape.1227) | copy-start | bytes 196612
  111.2 10.8 %copy-start.27 = (pred[2,2,1,1]{1,0,2,3:T(4,128)(4,1)S(1)}, pred[2,2,1,1]{1,0,2,3:T(4,128)(4,1)}, u32[]{:S(2)}) copy-start(pred[2,2,1,1]{1,0,2,3:T(4,128)(4,1)} %compare_bitcast_fusion) | copy-start | bytes 16
  111.2 11.7 %copy-start.12 = (f32[1,1,128,128]{2,3,1,0:T(8,128)S(1)}, f32[1,1,128,128]{2,3,1,0:T(8,128)}, u32[]{:S(2)}) copy-start(f32[1,1,128,128]{2,3,1,0:T(8,128)} %get-tuple-element.100) | copy-start | bytes 196612
  111.2 12.1 %copy-start = (f32[256,1024]{1,0:T(8,128)S(1)}, f32[256,1024]{1,0:T(8,128)}, u32[]{:S(2)}) copy-start(f32[256,1024]{1,0:T(8,128)} %param.4) | copy-start | bytes 3145732
  122.6 5.2 copy-start.26
  123.2 46.6 %copy-start.22 = (s32[5,32]{1,0:T(8,128)S(1)}, s32[5,32]{1,0:T(8,128)}, u32[]{:S(2)}) copy-start(s32[5,32]{1,0:T(8,128)} %param.7) | copy-start | bytes 1924
  126.6 455.3 %collective-permute-start = (f32[128,1024]{1,0:T(8,128)}, f32[128,1024]{1,0:T(8,128)}, u32[]{:S(2)}, u32[]{:S(2)}) collective-permute-start(f32[128,1024]{1,0:T(8,128)} %get-tuple-element.32), channel_id=1, source_target_pairs={{8,0},{16,8},{24,16},{32,24},{40,32},{48,40},{56,48},{64,56},{72,6... | collective-permute-start | bytes 1572872 | tf_op jit(solution)/shard_map/ppermute | solution.py:15
  200.2 13.3 %copy-start.25 = (f32[1,1,32,128]{3,2,1,0:T(8,128)S(1)}, f32[1,1,32,128]{3,2,1,0:T(8,128)}, u32[]{:S(2)}) copy-start(f32[1,1,32,128]{3,2,1,0:T(8,128)} %get-tuple-element.37) | copy-start | bytes 49156
  281.8 14.5 %copy-start.24 = (f32[1,1,32,128]{3,2,1,0:T(8,128)S(1)}, f32[1,1,32,128]{3,2,1,0:T(8,128)}, u32[]{:S(2)}) copy-start(f32[1,1,32,128]{3,2,1,0:T(8,128)} %get-tuple-element.34) | copy-start | bytes 49156
  366.6 13.3 %copy-start.23 = (f32[1,1,32,128]{3,2,1,0:T(8,128)S(1)}, f32[1,1,32,128]{3,2,1,0:T(8,128)}, u32[]{:S(2)}) copy-start(f32[1,1,32,128]{3,2,1,0:T(8,128)} %get-tuple-element.35) | copy-start | bytes 49156
  487.0 27.3 %copy-start.3 = (pred[8,8,1,1]{1,0,2,3:T(8,128)(4,1)S(1)}, pred[8,8,1,1]{1,0,2,3:T(8,128)(4,1)}, u32[]{:S(2)}) copy-start(pred[8,8,1,1]{1,0,2,3:T(8,128)(4,1)} %fusion.286) | copy-start | bytes 196
  493.6 26.0 %copy-start.6 = (pred[4,4,1,1]{1,0,2,3:T(4,128)(4,1)S(1)}, pred[4,4,1,1]{1,0,2,3:T(4,128)(4,1)}, u32[]{:S(2)}) copy-start(pred[4,4,1,1]{1,0,2,3:T(4,128)(4,1)} %fusion.287) | copy-start | bytes 52
  536.7 15.8 %copy-start.4 = (pred[8,8,1,1]{1,0,2,3:T(8,128)(4,1)S(1)}, pred[8,8,1,1]{1,0,2,3:T(8,128)(4,1)}, u32[]{:S(2)}) copy-start(pred[8,8,1,1]{1,0,2,3:T(8,128)(4,1)} %fusion.286) | copy-start | bytes 196
  553.9 22.6 %copy-start.5 = (pred[8,8,1,1]{1,0,2,3:T(8,128)(4,1)S(1)}, pred[8,8,1,1]{1,0,2,3:T(8,128)(4,1)}, u32[]{:S(2)}) copy-start(pred[8,8,1,1]{1,0,2,3:T(8,128)(4,1)} %fusion.286) | copy-start | bytes 196
  561.1 16.5 %copy-start.7 = (pred[4,4,1,1]{1,0,2,3:T(4,128)(4,1)S(1)}, pred[4,4,1,1]{1,0,2,3:T(4,128)(4,1)}, u32[]{:S(2)}) copy-start(pred[4,4,1,1]{1,0,2,3:T(4,128)(4,1)} %fusion.287) | copy-start | bytes 52
  569.6 11.4 %copy-start.13 = (f32[1,2,32,32]{3,2,1,0:T(8,128)S(1)}, f32[1,2,32,32]{3,2,1,0:T(8,128)}, u32[]{:S(2)}) copy-start(f32[1,2,32,32]{3,2,1,0:T(8,128)} %fusion.5) | copy-start | bytes 24580
  569.6 11.4 %copy-start.16 = (f32[1,2,32,32]{3,2,1,0:T(8,128)S(1)}, f32[1,2,32,32]{3,2,1,0:T(8,128)}, u32[]{:S(2)}) copy-start(f32[1,2,32,32]{3,2,1,0:T(8,128)} %get-tuple-element.43) | copy-start | bytes 24580
  569.6 11.4 %copy-start.17 = (f32[1,2,32,32]{3,2,1,0:T(8,128)S(1)}, f32[1,2,32,32]{3,2,1,0:T(8,128)}, u32[]{:S(2)}) copy-start(f32[1,2,32,32]{3,2,1,0:T(8,128)} %get-tuple-element.44) | copy-start | bytes 24580
  569.6 11.5 %copy-start.14 = (f32[1,2,32,32]{3,2,1,0:T(8,128)S(1)}, f32[1,2,32,32]{3,2,1,0:T(8,128)}, u32[]{:S(2)}) copy-start(f32[1,2,32,32]{3,2,1,0:T(8,128)} %fusion.10) | copy-start | bytes 24580
  569.6 11.5 %copy-start.18 = (f32[1,2,32,32]{3,2,1,0:T(8,128)S(1)}, f32[1,2,32,32]{3,2,1,0:T(8,128)}, u32[]{:S(2)}) copy-start(f32[1,2,32,32]{3,2,1,0:T(8,128)} %get-tuple-element.58) | copy-start | bytes 24580
  569.6 11.5 %copy-start.19 = (f32[1,2,32,32]{3,2,1,0:T(8,128)S(1)}, f32[1,2,32,32]{3,2,1,0:T(8,128)}, u32[]{:S(2)}) copy-start(f32[1,2,32,32]{3,2,1,0:T(8,128)} %get-tuple-element.59) | copy-start | bytes 24580
  569.6 11.6 %copy-start.15 = (f32[1,2,32,32]{3,2,1,0:T(8,128)S(1)}, f32[1,2,32,32]{3,2,1,0:T(8,128)}, u32[]{:S(2)}) copy-start(f32[1,2,32,32]{3,2,1,0:T(8,128)} %fusion.15) | copy-start | bytes 24580
  569.6 11.6 %copy-start.20 = (f32[1,2,32,32]{3,2,1,0:T(8,128)S(1)}, f32[1,2,32,32]{3,2,1,0:T(8,128)}, u32[]{:S(2)}) copy-start(f32[1,2,32,32]{3,2,1,0:T(8,128)} %get-tuple-element.73) | copy-start | bytes 24580
  569.6 11.6 %copy-start.21 = (f32[1,2,32,32]{3,2,1,0:T(8,128)S(1)}, f32[1,2,32,32]{3,2,1,0:T(8,128)}, u32[]{:S(2)}) copy-start(f32[1,2,32,32]{3,2,1,0:T(8,128)} %get-tuple-element.74) | copy-start | bytes 24580
  569.7 11.8 %copy-start.11 = (f32[1,1,128,128]{2,3,1,0:T(8,128)S(1)}, f32[1,1,128,128]{2,3,1,0:T(8,128)}, u32[]{:S(2)}) copy-start(f32[1,1,128,128]{2,3,1,0:T(8,128)} %get-tuple-element.85) | copy-start | bytes 196612
  581.2 5.3 copy-start.10
  586.4 15.0 %copy-start.9 = (f32[1,1,128,128]{2,3,1,0:T(8,128)S(1)}, f32[1,1,128,128]{2,3,1,0:T(8,128)}, u32[]{:S(2)}) copy-start(f32[1,1,128,128]{2,3,1,0:T(8,128)} %get-tuple-element.55) | copy-start | bytes 196612
  586.5 12.3 %collective-permute-start.1 = (f32[128,1024]{1,0:T(8,128)S(1)}, f32[128,1024]{1,0:T(8,128)S(1)}, u32[]{:S(2)}, u32[]{:S(2)}) collective-permute-start(f32[128,1024]{1,0:T(8,128)S(1)} %get-tuple-element.29), channel_id=1, source_target_pairs={{248,0},{0,8},{8,16},{16,24},{24,32},{32,40},{40,48},{48,56},{56,6... | collective-permute-start | bytes 1572872 | tf_op jit(solution)/shard_map/ppermute | solution.py:15
  601.2 9.5 %copy-start.8 = (f32[1,1,128,128]{2,3,1,0:T(8,128)S(1)}, f32[1,1,128,128]{2,3,1,0:T(8,128)}, u32[]{:S(2)}) copy-start(f32[1,1,128,128]{2,3,1,0:T(8,128)} %get-tuple-element.40) | copy-start | bytes 196612
  601.2 7.0 %collective-permute-start.2 = (f32[128,1024]{1,0:T(8,128)S(1)}, f32[128,1024]{1,0:T(8,128)S(1)}, u32[]{:S(2)}, u32[]{:S(2)}) collective-permute-start(f32[128,1024]{1,0:T(8,128)S(1)} %get-tuple-element.28), channel_id=1, source_target_pairs={{8,0},{16,8},{24,16},{32,24},{40,32},{48,40},{56,48},{64,56},{72,6... | collective-permute-start | bytes 1572872 | tf_op jit(solution)/shard_map/ppermute | solution.py:15
  610.6 12.5 %collective-permute-start.3 = (f32[128,1024]{1,0:T(8,128)S(1)}, f32[128,1024]{1,0:T(8,128)S(1)}, u32[]{:S(2)}, u32[]{:S(2)}) collective-permute-start(f32[128,1024]{1,0:T(8,128)S(1)} %get-tuple-element.25), channel_id=1, source_target_pairs={{248,0},{0,8},{8,16},{16,24},{24,32},{32,40},{40,48},{48,56},{56,6... | collective-permute-start | bytes 1572872 | tf_op jit(solution)/shard_map/ppermute | solution.py:15
where the time goes:
time: 637 us; the launch traced here: 627 us
  blocking collectives  344 us (54%)
  local copies, waits for them, and re-layouts  129 us (20%)
  matrix products  97.3 us (15%)
  waiting for transfers between devices  30 us (5%)
  other arithmetic  20.2 us (3%)
    all_gather x5, blocking collectives, on_device(): gathered = lax.all_gather(stored, 'row', axis=0, tiled=True)  203 us
    all_gather x5, blocking collectives, on_device(): reflect = lax.all_gather(my_panel, 'col', axis=1, tiled=True)  141 us
    another operation x65, local copies, waits for them, and re-layouts  97.2 us
    dot_general x30, matrix products, invert_upper(): paired = jnp.einsum('gpaqb,pq->gpab', grouped, picker, precision=PRECISE)  51.9 us
    ppermute x4, waiting for transfers between devices, passed_along(): return lax.ppermute(block, axis, route)  30 us
    concatenate x25, other arithmetic, invert_upper(): blocks = jnp.concatenate([top_rows, bottom], axis=2)  13 us
  transfers between devices with their start and end apart: 4, of which 3 were waited for; matrix products, arithmetic and copies ran while one was open for 29% of the time, Pallas kernels for 0%

commit v1 on v0

v1 whole, which is shorter than its diff:
```python
import functools

import jax
import jax.numpy as jnp
from jax import lax
from jax.experimental import pallas as pl
from jax.experimental.pallas import tpu as pltpu
from jax.sharding import PartitionSpec as P

MESH = pl.DeviceIdType.MESH
F32, BF16 = jnp.float32, jnp.bfloat16
B = 128
SWEEPS = 5
ROWS, COLS = 32, 8
RING = 8
PIECE = 32
GROUPS = ((0, 1), (1, 3), (3, 5))
WINDOWS = ((0, 0), (1, 0), (1, 1), (2, 0), (3, 0), (3, 1), (4, 0))
CHUNK = 256
CHUNKS = 1024 // CHUNK


def copy_ids():
    ids = {}
    for g in range(len(GROUPS)):
        names = [("across", g)]
        names += [("up", g, 1, item) for item in (0, 1)] + [("down", g, 1, item) for item in (0, 1)]
        names += [("up", g, t) for t in (2, 3, 4)] + [("down", g, t) for t in (2, 3)]
        names += [("mate", g, "own", item) for item in (0, 1)]
        names += [("mate", g, "up", t) for t in (1, 2, 3, 4)] + [("mate", g, "down", t) for t in (1, 2, 3)]
        for name in names:
            ids[name] = len(ids)
    for w in range(len(WINDOWS)):
        for j in range(1, COLS):
            ids[("col", w, j)] = len(ids)
    for x in (0, 1):
        for side in ("prev", "next"):
            for j in range(CHUNKS):
                ids[(side, x, j)] = len(ids)
    return ids


IDS = copy_ids()


def split(a):
    high = a.astype(BF16)
    return high, (a - high.astype(F32)).astype(BF16)


def dot3(a, b, dims=((1,), (0,))):
    (ah, al), (bh, bl) = a, b
    dot = lambda x, y: lax.dot_general(x, y, (dims, ((), ())), preferred_element_type=F32)
    return dot(ah, bh) + (dot(ah, bl) + dot(al, bh))


def dot6(a, b, dims=((1,), (0,))):
    return lax.dot_general(a, b, (dims, ((), ())), precision=lax.Precision.HIGHEST, preferred_element_type=F32)


def inverse(products):
    row = lax.broadcasted_iota(jnp.int32, (B, B), 0)
    col = lax.broadcasted_iota(jnp.int32, (B, B), 1)
    diagonal = jnp.where(row == col, products, 0.0)
    down = 2.0 / jnp.sum(diagonal, axis=1, keepdims=True)
    along = 2.0 / jnp.sum(diagonal, axis=0, keepdims=True)
    first = (col == row + 1) & ((row & 1) == 0)
    inv = jnp.where(row == col, down, 0.0) - jnp.where(first, down * products * along, 0.0)
    width = 2
    while width < B:
        pair = 2 * width
        corner = ((row & -pair) == (col & -pair)) & ((row & width) == 0) & ((col & width) != 0)
        off = jnp.where(corner, products, 0.0)
        inv = inv - dot6(dot6(inv, off), inv)
        width = pair
    return inv


def reflector(panel_ref):
    panel = panel_ref[...]
    inv = inverse(dot6(panel, panel, ((0,), (0,))))
    v = split(panel)
    return v, dot3(v, split(inv))


def transform(v, vt, top):
    rows = slice(0, B) if top else slice(B, 2 * B)
    row = lax.broadcasted_iota(jnp.int32, (B, 2 * B), 0) + (0 if top else B)
    col = lax.broadcasted_iota(jnp.int32, (B, 2 * B), 1)
    ident = jnp.where(row == col, 1.0, 0.0)
    return split(ident - dot3(split(vt[rows]), v, ((1,), (1,))))


def kernel(
    z_ref, panels, shift, slots, out_ref,
    gathered, stage, full, first, second, from_prev, from_next, hh, hl, send_sem, recv_sem,
):
    r, c = lax.axis_index("row"), lax.axis_index("col")
    k = lax.rem(r, 2)
    z = lax.rem(lax.div(r, 2), RING)
    h = lax.div(r, 2 * RING)
    row_of = lambda h_, z_, k_: (h_ * RING + z_) * 2 + k_
    ring = lambda d: lax.rem(z + d + RING, RING)
    up, down = row_of(h, ring(1), k), row_of(h, ring(-1), k)
    mate, across = row_of(h, z, 1 - k), row_of(1 - h, z, k)
    prev_row, next_row = lax.rem(r + ROWS - 1, ROWS), lax.rem(r + 1, ROWS)
    other_col = lambda j: lax.rem(c + j + COLS, COLS)
    sent = []

    def send(name, src, dst, row, col):
        i = IDS[name]
        copy = pltpu.make_async_remote_copy(
            src_ref=src, dst_ref=dst, send_sem=send_sem.at[i], recv_sem=recv_sem.at[i],
            device_id=(row, col), device_id_type=MESH,
        )
        copy.start()
        sent.append(copy)

    def arrive(name, dst):
        i = IDS[name]
        pltpu.make_async_remote_copy(
            src_ref=dst, dst_ref=dst, send_sem=send_sem.at[i], recv_sem=recv_sem.at[i],
            device_id=(mate, c), device_id_type=MESH,
        ).wait_recv()

    barrier = pltpu.get_barrier_semaphore()
    partners = [(up, c), (down, c), (mate, c), (across, c), (prev_row, c), (next_row, c)]
    partners += [(r, other_col(j)) for j in range(1, COLS)]
    for partner in partners:
        pl.semaphore_signal(barrier, inc=1, device_id=partner, device_id_type=MESH)
    pl.semaphore_wait(barrier, len(partners))

    spans = [pl.ds(a, b - a) for a, b in GROUPS]
    for g, span in enumerate(spans):
        own = gathered.at[span, k, z, h]
        send(("across", g), panels.at[span], own, across, c)
        send(("up", g, 1, 0), panels.at[span], own, up, c)
        send(("down", g, 1, 0), panels.at[span], own, down, c)
        send(("mate", g, "own", 0), panels.at[span], own, mate, c)
    for s in range(SWEEPS):
        gathered[s, k, z, h] = panels[s]
    for g, span in enumerate(spans):
        other = gathered.at[span, k, z, 1 - h]
        arrive(("across", g), other)
        send(("up", g, 1, 1), other, other, up, c)
        send(("down", g, 1, 1), other, other, down, c)
        send(("mate", g, "own", 1), other, other, mate, c)
    for t in (1, 2, 3, 4):
        for g, span in enumerate(spans):
            for side, sign, steps, onward in (("up", -1, 4, up), ("down", 1, 3, down)):
                if t > steps:
                    continue
                at = ring(sign * t)
                block = gathered.at[span, k, at]
                if t == 1:
                    arrive((side, g, 1, 0), gathered.at[span, k, at, h])
                    arrive((side, g, 1, 1), gathered.at[span, k, at, 1 - h])
                else:
                    arrive((side, g, t), block)
                if t < steps:
                    send((side, g, t + 1), block, block, onward, c)
                send(("mate", g, side, t), block, block, mate, c)
    for g, span in enumerate(spans):
        arrive(("mate", g, "own", 0), gathered.at[span, 1 - k, z, h])
        arrive(("mate", g, "own", 1), gathered.at[span, 1 - k, z, 1 - h])
        for side, sign, steps in (("up", -1, 4), ("down", 1, 3)):
            for t in range(1, steps + 1):
                arrive(("mate", g, side, t), gathered.at[span, 1 - k, ring(sign * t)])

    for w, (s, back) in enumerate(WINDOWS):
        wanted = lax.rem(r + 2 * ROWS - back - shift[s], ROWS)
        slot = jnp.int32(0)
        for p in range(ROWS):
            slot = jnp.where(slots[s, p] == wanted, p, slot)
        piece = gathered[s, lax.rem(slot, 2), lax.rem(lax.div(slot, 2), RING), lax.div(slot, 2 * RING)]
        stage[w] = piece
        full[w, pl.ds(pl.multiple_of(c * PIECE, PIECE), PIECE)] = piece
    for w in range(len(WINDOWS)):
        place = full.at[w, pl.ds(pl.multiple_of(c * PIECE, PIECE), PIECE)]
        for j in range(1, COLS):
            send(("col", w, j), stage.at[w], place, r, other_col(j))

    def wait_panel(w):
        for j in range(1, COLS):
            arrive(("col", w, j), full.at[w, pl.ds(pl.multiple_of(other_col(-j) * PIECE, PIECE), PIECE)])

    def make_transform(s):
        found = [w for w, (of, _) in enumerate(WINDOWS) if of == s]
        for w in found:
            wait_panel(w)
        for half in (0, 1):
            w = found[0] if half == 0 else found[-1]
            if half == 0 or len(found) == 2:
                v, vt = reflector(full.at[w])
            hh[s, half], hl[s, half] = transform(v, vt, half == 0)

    def times(s, half, top, bottom):
        a = (hh[s, half, :, :B], hl[s, half, :, :B])
        b = (hh[s, half, :, B:], hl[s, half, :, B:])
        return dot3(a, split(top)) + dot3(b, split(bottom))

    def exchange(x, j, block):
        send(("prev", x, j), block.at[j, pl.ds(0, B)], from_next.at[x, j], prev_row, c)
        send(("next", x, j), block.at[j, pl.ds(B, B)], from_prev.at[x, j], next_row, c)

    def odd_even(x, j, block):
        s = 2 * x + 1
        arrive(("prev", x, j), from_next.at[x, j])
        arrive(("next", x, j), from_prev.at[x, j])
        high = times(s, 0, block[j, B:], from_next[x, j])
        low = times(s, 1, from_prev[x, j], block[j, :B])
        return times(s + 1, 0, low, high), times(s + 1, 1, low, high)

    make_transform(0)
    for j in range(CHUNKS):
        cols = slice(j * CHUNK, (j + 1) * CHUNK)
        for half in (0, 1):
            first[j, half * B : half * B + B] = times(0, half, z_ref[:B, cols], z_ref[B:, cols])
        if j:
            exchange(0, j - 1, first)
    make_transform(1)
    exchange(0, CHUNKS - 1, first)
    make_transform(2)
    for j in range(CHUNKS):
        second[j, :B], second[j, B:] = odd_even(0, j, first)
        if j:
            exchange(1, j - 1, second)
    make_transform(3)
    exchange(1, CHUNKS - 1, second)
    make_transform(4)
    for j in range(CHUNKS):
        cols = slice(j * CHUNK, (j + 1) * CHUNK)
        out_ref[:B, cols], out_ref[B:, cols] = odd_even(1, j, second)
    for copy in sent:
        copy.wait_send()


def on_device(eigvecs, panels, sweep_shift, slot_group):
    rows, cols = eigvecs.shape
    vmem, smem = pl.BlockSpec(memory_space=pltpu.VMEM), pl.BlockSpec(memory_space=pltpu.SMEM)
    return pl.pallas_call(
        kernel,
        out_shape=jax.ShapeDtypeStruct((rows, cols), F32),
        in_specs=[vmem, vmem, smem, smem],
        out_specs=vmem,
        scratch_shapes=[
            pltpu.VMEM((SWEEPS, 2, RING, 2, PIECE, B), F32),
            pltpu.VMEM((len(WINDOWS), PIECE, B), F32),
            pltpu.VMEM((len(WINDOWS), 2 * B, B), F32),
            pltpu.VMEM((CHUNKS, 2 * B, CHUNK), F32),
            pltpu.VMEM((CHUNKS, 2 * B, CHUNK), F32),
            pltpu.VMEM((2, CHUNKS, B, CHUNK), F32),
            pltpu.VMEM((2, CHUNKS, B, CHUNK), F32),
            pltpu.VMEM((SWEEPS, 2, B, 2 * B), BF16),
            pltpu.VMEM((SWEEPS, 2, B, 2 * B), BF16),
            pltpu.SemaphoreType.DMA((len(IDS),)),
            pltpu.SemaphoreType.DMA((len(IDS),)),
        ],
        compiler_params=pltpu.CompilerParams(collective_id=0, has_side_effects=True),
    )(eigvecs, panels.reshape(SWEEPS, PIECE, B), sweep_shift, slot_group)


def solution(mesh):
    in_specs = (P("row", "col"), P(None, "row", "col", None), P(), P())
    return jax.shard_map(on_device, mesh=mesh, in_specs=in_specs, out_specs=P("row", "col"), check_vma=False)
```

time: 637 us -> 72.1 us (0.11)
  the two profiles are of different devices: /device:TPU:24 before, /device:TPU:1 now
where the time goes in v1:
time: 72.1 us; the launch traced here: 71.9 us
  Pallas kernels  69.6 us (97%)
  local copies, waits for them, and re-layouts  2.31 us (3%)
    pallas_call x1, Pallas kernels, on_device(): pl.pallas_call(kernel, out_shape=jax.ShapeDtypeStruct((rows, cols), F32),...  69.6 us
    unnamed x1, local copies, waits for them, and re-layouts  2.31 us

profile of v1, /device:TPU:1, one launch (start us, length us, event | category | flops | bytes accessed | tf_op | source)
XLA Modules:
  0.0 71.9 jit_solution(3144914642232686917)
XLA Ops:
  0.0 69.6 %shard_map.46 = f32[256,1024]{1,0:T(8,128)} custom-call(f32[256,1024]{1,0:T(8,128)} %z_ref.1, f32[5,32,128]{2,1,0:T(8,128)} %bitcast.1, s32[5]{0:T(128)} %shift.1, s32[5,32]{1,0:T(8,128)} %slots.1), custom_call_target="tpu_custom_call" | custom-call | tf_op jit(solution)/shard_map/pallas_call | solution.py:241
  69.6 2.3 %copy.6 = f32[256,1024]{1,0:T(8,128)} copy(f32[256,1024]{1,0:T(8,128)} %shard_map.46) | data formatting | bytes 2097152

commit v2 on v0

v2 whole, which is shorter than its diff:
```python
import jax
import jax.numpy as jnp
from jax import lax
from jax.experimental import pallas as pl
from jax.experimental.pallas import tpu as pltpu
from jax.sharding import PartitionSpec as P

MESH = pl.DeviceIdType.MESH
F32, BF16 = jnp.float32, jnp.bfloat16
B = 128
SWEEPS = 5
ROWS, COLS = 32, 8
RING = 8
PIECE = 32
WINDOWS = ((0, 0), (1, 0), (1, 1), (2, 0), (3, 0), (3, 1), (4, 0))
LATER = len(WINDOWS) - 1
CHUNK = 256
CHUNKS = 1024 // CHUNK
COPIES = 160


def split(a):
    high = a.astype(BF16)
    return high, (a - high.astype(F32)).astype(BF16)


def dot3(a, b, dims=((1,), (0,))):
    (ah, al), (bh, bl) = a, b
    dot = lambda x, y: lax.dot_general(x, y, (dims, ((), ())), preferred_element_type=F32)
    return dot(ah, bh) + (dot(ah, bl) + dot(al, bh))


def dot6(a, b, dims=((1,), (0,))):
    return lax.dot_general(a, b, (dims, ((), ())), precision=lax.Precision.HIGHEST, preferred_element_type=F32)


def inverses(grams):
    row = lax.broadcasted_iota(jnp.int32, (B, B), 0)
    col = lax.broadcasted_iota(jnp.int32, (B, B), 1)
    first = (col == row + 1) & ((row & 1) == 0)

    def start(gram):
        diagonal = jnp.where(row == col, gram, 0.0)
        down = 2.0 / jnp.sum(diagonal, axis=1, keepdims=True)
        along = 2.0 / jnp.sum(diagonal, axis=0, keepdims=True)
        return jnp.where(row == col, down, 0.0) - jnp.where(first, down * gram * along, 0.0)

    invs = [start(gram) for gram in grams]
    width = 2
    while width < B:
        pair = 2 * width
        corner = ((row & -pair) == (col & -pair)) & ((row & width) == 0) & ((col & width) != 0)
        offs = [jnp.where(corner, gram, 0.0) for gram in grams]
        if width < 8:
            inner = [dot6(inv, off) for inv, off in zip(invs, offs)]
            invs = [inv - dot6(part, inv) for part, inv in zip(inner, invs)]
        else:
            parts = [inv.reshape(B // pair, pair, B) for inv in invs]
            uppers = [part[:, :width].reshape(B // 2, B) for part in parts]
            inner = [dot6(upper, off) for upper, off in zip(uppers, offs)]
            uppers = [upper - dot6(part, inv) for upper, part, inv in zip(uppers, inner, invs)]
            invs = [
                jnp.concatenate([upper.reshape(B // pair, width, B), part[:, width:]], axis=1).reshape(B, B)
                for upper, part in zip(uppers, parts)
            ]
        width = pair
    return invs


def reflectors(panels):
    invs = inverses([dot6(panel, panel, ((0,), (0,))) for panel in panels])
    vs = [split(panel) for panel in panels]
    return [(v, dot3(v, split(inv))) for v, inv in zip(vs, invs)]


def transform(reflector, top):
    v, vt = reflector
    rows = slice(0, B) if top else slice(B, 2 * B)
    row = lax.broadcasted_iota(jnp.int32, (B, 2 * B), 0) + (0 if top else B)
    col = lax.broadcasted_iota(jnp.int32, (B, 2 * B), 1)
    return split(jnp.where(row == col, 1.0, 0.0) - dot3(split(vt[rows]), v, ((1,), (1,))))


def kernel(
    z_hbm, panels_hbm, shift, slots, out_hbm,
    z_in, panels, gathered0, gathered1, gathered2, gathered3, gathered4, stage, wanted0,
    far_out, far_in1, far_in2, far_in3, far_in4, full, blocks, outs, hh, hl, send_sem, recv_sem, own_sem,
):
    gathered, far_in = (gathered0, gathered1, gathered2, gathered3, gathered4), (far_in1, far_in2, far_in3, far_in4)
    r, c = lax.axis_index("row"), lax.axis_index("col")
    k = lax.rem(r, 2)
    z = lax.rem(lax.div(r, 2), RING)
    h = lax.div(r, 2 * RING)
    row_of = lambda h_, z_, k_: (h_ * RING + z_) * 2 + k_
    ring = lambda d: lax.rem(z + d + RING, RING)
    ring_row = lambda d: row_of(h, ring(d), k)
    mate, across = row_of(h, z, 1 - k), row_of(1 - h, z, k)
    prev_row, next_row = lax.rem(r + ROWS - 1, ROWS), lax.rem(r + 1, ROWS)
    other_col = lambda j: lax.rem(c + j + COLS, COLS)
    strip = lambda col: pl.ds(pl.multiple_of(col * PIECE, PIECE), PIECE)
    ids, sent = {}, []

    def remote(name, src, dst, row, col):
        i = ids.setdefault(name, len(ids))
        return pltpu.make_async_remote_copy(
            src_ref=src, dst_ref=dst, send_sem=send_sem.at[i], recv_sem=recv_sem.at[i],
            device_id=(row, col), device_id_type=MESH,
        )

    def send(name, src, dst, row, col):
        copy = remote(name, src, dst, row, col)
        copy.start()
        sent.append(copy)

    def arrive(name, dst):
        remote(name, dst, dst, mate, c).wait_recv()

    barrier = pltpu.get_barrier_semaphore()
    partners = [(ring_row(d), c) for d in range(1, RING)] + [(mate, c), (prev_row, c), (next_row, c)]
    everyone = [(flip, j) for flip in (0, 1) for j in range(COLS) if (flip, j) != (0, 0)]
    partners += [(across if flip else r, other_col(j)) for flip, j in everyone]
    for partner in partners:
        pl.semaphore_signal(barrier, inc=1, device_id=partner, device_id_type=MESH)
    panels_copy = pltpu.make_async_copy(panels_hbm, panels, own_sem.at[0])
    panels_copy.start()
    z_copy = pltpu.make_async_copy(z_hbm, z_in, own_sem.at[1])
    z_copy.start()
    pl.semaphore_wait(barrier, len(partners))
    panels_copy.wait()

    def ring_send(s):
        for d in (4, 3, 5, 2, 6, 1, 7):
            send(("ring", s, d), panels.at[s], gathered[s].at[k, z], ring_row(d), c)
        send(("mate", s, 0), panels.at[s], gathered[s].at[k, z], mate, c)

    def receive(s, distances):
        for d in distances:
            block = gathered[s].at[k, ring(-d)]
            arrive(("ring", s, d), block)
            send(("mate", s, d), block, block, mate, c)

    def receive_mate(s):
        for d in range(RING):
            arrive(("mate", s, d), gathered[s].at[1 - k, ring(-d)])

    near, distant = (1, 7, 2, 6), (3, 5, 4)
    ring_send(0)
    for s in range(SWEEPS):
        gathered[s][k, z] = panels[s]

    def find(s, row):
        wanted = lax.rem(row + 2 * ROWS - shift[s], ROWS)
        slot = jnp.int32(0)
        for p in range(ROWS):
            slot = jnp.where(slots[s, p] == wanted, p, slot)
        return lax.div(slot, 2 * RING), (lax.rem(slot, 2), lax.rem(lax.div(slot, 2), RING))

    halves, places = zip(*[find(s, r - back) for s, back in WINDOWS])
    _, places_across = zip(*[find(s, across - back) for s, back in WINDOWS])
    receive(0, near)
    ring_send(1)
    receive(0, distant)
    receive_mate(0)
    stage[0] = gathered[0][places[0]]
    far_out[0] = gathered[0][places_across[0]]
    wanted0[h, strip(c)] = gathered[0][places[0]]
    ring_send(2)
    for flip, j in everyone:
        source = far_out if flip else stage
        send(("first share", flip, j), source.at[0], wanted0.at[h, strip(c)], across if flip else r, other_col(j))

    of_sweep = [[w for w, (of, _) in enumerate(WINDOWS) if of == s] for s in range(SWEEPS)]

    def cross(s):
        receive_mate(s)
        ws = of_sweep[s]
        for w in ws:
            far_out[w] = gathered[s][places_across[w]]
        span = pl.ds(ws[0], len(ws))
        send(("far", s), far_out.at[span], far_in[s - 1].at[pl.ds(0, len(ws))], across, c)

    def share(s):
        ws = of_sweep[s]
        arrive(("far", s), far_in[s - 1].at[pl.ds(0, len(ws))])
        for i, w in enumerate(ws):
            piece = jnp.where(halves[w] == h, gathered[s][places[w]], far_in[s - 1][i])
            stage[w] = piece
            full[w - 1, strip(c)] = piece
        for w in ws:
            for j in range(1, COLS):
                send(("share", w, j), stage.at[w], full.at[w - 1, strip(c)], r, other_col(j))

    receive(1, near)
    ring_send(3)
    receive(1, distant)
    cross(1)
    receive(2, near)
    ring_send(4)
    receive(2, distant)
    cross(2)

    for flip, j in everyone:
        arrive(("first share", flip, j), wanted0.at[1 - h if flip else h, strip(other_col(-j))])
    share(1)
    (first,) = reflectors([wanted0[halves[0]]])
    hh[0, :B], hl[0, :B] = transform(first, True)
    hh[0, B:], hl[0, B:] = transform(first, False)
    share(2)
    receive(3, near + distant)
    cross(3)
    z_copy.wait()

    def times(s, rows, block):
        return dot3((hh[s, rows], hl[s, rows]), block)

    low, high, both = slice(0, B), slice(B, 2 * B), slice(0, 2 * B)

    def exchange(x, j):
        mine = blocks.at[x, j]
        send(("prev", x, j), mine.at[pl.ds(B, B)], mine.at[pl.ds(3 * B, B)], prev_row, c)
        send(("next", x, j), mine.at[pl.ds(2 * B, B)], mine.at[pl.ds(0, B)], next_row, c)

    def odd_even(x, j):
        s = 2 * x + 1
        mine = blocks.at[x, j]
        arrive(("prev", x, j), mine.at[pl.ds(3 * B, B)])
        arrive(("next", x, j), mine.at[pl.ds(0, B)])
        new_low = times(s, low, split(mine[0 : 2 * B]))
        new_high = times(s, high, split(mine[2 * B : 4 * B]))
        return times(s + 1, both, split(jnp.concatenate([new_low, new_high], axis=0)))

    def transforms(ws):
        s = WINDOWS[ws[0]][0]
        for w in ws:
            for j in range(1, COLS):
                arrive(("share", w, j), full.at[w - 1, strip(other_col(-j))])
        own, back, even = reflectors([full[w - 1] for w in ws])
        hh[s, low], hl[s, low] = transform(back, False)
        hh[s, high], hl[s, high] = transform(own, True)
        hh[s + 1, low], hl[s + 1, low] = transform(even, True)
        hh[s + 1, high], hl[s + 1, high] = transform(even, False)

    for j in range(CHUNKS):
        cols = slice(j * CHUNK, (j + 1) * CHUNK)
        blocks[0, j, B : 3 * B] = times(0, both, split(z_in[:, cols]))
        if j:
            exchange(0, j - 1)
    receive(4, near + distant)
    exchange(0, CHUNKS - 1)
    cross(4)
    share(3)
    transforms((1, 2, 3))
    share(4)
    for j in range(CHUNKS):
        blocks[1, j, B : 3 * B] = odd_even(0, j)
        if j:
            exchange(1, j - 1)
    z_in[0:8, 0:B] = jnp.zeros((8, B), F32)
    exchange(1, CHUNKS - 1)
    transforms((4, 5, 6))
    out_copies = []
    for j in range(CHUNKS):
        outs[j] = odd_even(1, j)
        cols = pl.ds(j * CHUNK, CHUNK)
        out_copies.append(pltpu.make_async_copy(outs.at[j], out_hbm.at[:, cols], own_sem.at[2 + j]))
        out_copies[-1].start()
    for copy in sent:
        copy.wait_send()
    for copy in out_copies:
        copy.wait()


def on_device(eigvecs, panels, sweep_shift, slot_group):
    rows, cols = eigvecs.shape
    hbm, smem = pl.BlockSpec(memory_space=pl.ANY), pl.BlockSpec(memory_space=pltpu.SMEM)
    return pl.pallas_call(
        kernel,
        out_shape=jax.ShapeDtypeStruct((rows, cols), F32),
        in_specs=[hbm, hbm, smem, smem],
        out_specs=hbm,
        scratch_shapes=[
            pltpu.VMEM((rows, cols), F32),
            pltpu.VMEM((SWEEPS, PIECE, B), F32),
            *[pltpu.VMEM((2, RING, PIECE, B), F32)] * SWEEPS,
            pltpu.VMEM((len(WINDOWS), PIECE, B), F32),
            pltpu.VMEM((2, 2 * B, B), F32),
            pltpu.VMEM((len(WINDOWS), PIECE, B), F32),
            *[pltpu.VMEM((2, PIECE, B), F32)] * (SWEEPS - 1),
            pltpu.VMEM((LATER, 2 * B, B), F32),
            pltpu.VMEM((2, CHUNKS, 4 * B, CHUNK), F32),
            pltpu.VMEM((CHUNKS, 2 * B, CHUNK), F32),
            pltpu.VMEM((SWEEPS, 2 * B, 2 * B), BF16),
            pltpu.VMEM((SWEEPS, 2 * B, 2 * B), BF16),
            pltpu.SemaphoreType.DMA((COPIES,)),
            pltpu.SemaphoreType.DMA((COPIES,)),
            pltpu.SemaphoreType.DMA((2 + CHUNKS,)),
        ],
        compiler_params=pltpu.CompilerParams(collective_id=0, has_side_effects=True),
    )(eigvecs, panels.reshape(SWEEPS, PIECE, B), sweep_shift, slot_group)


def solution(mesh):
    in_specs = (P("row", "col"), P(None, "row", "col", None), P(), P())
    return jax.shard_map(on_device, mesh=mesh, in_specs=in_specs, out_specs=P("row", "col"), check_vma=False)
```

time: 637 us -> 63.2 us (0.10)
  the two profiles are of different devices: /device:TPU:24 before, /device:TPU:2 now
where the time goes in v2:
time: 63.2 us; the launch traced here: 63.1 us
  Pallas kernels  60.8 us (96%)
  local copies, waits for them, and re-layouts  2.31 us (4%)
    pallas_call x1, Pallas kernels, on_device(): pl.pallas_call(kernel, out_shape=jax.ShapeDtypeStruct((rows, cols), F32),...  60.8 us
    unnamed x1, local copies, waits for them, and re-layouts  2.31 us

profile of v2, /device:TPU:2, one launch (start us, length us, event | category | flops | bytes accessed | tf_op | source)
XLA Modules:
  0.0 63.1 jit_solution(7471223950450597413)
XLA Ops:
  0.0 60.8 %shard_map.46 = f32[256,1024]{1,0:T(8,128)} custom-call(f32[256,1024]{1,0:T(8,128)} %z_hbm.1, f32[5,32,128]{2,1,0:T(8,128)} %bitcast.1, s32[5]{0:T(128)} %shift.1, s32[5,32]{1,0:T(8,128)} %slots.1), custom_call_target="tpu_custom_call" | custom-call | tf_op jit(solution)/shard_map/pallas_call | solution.py:276
  60.8 2.3 %copy.6 = f32[256,1024]{1,0:T(8,128)} copy(f32[256,1024]{1,0:T(8,128)} %shard_map.46) | data formatting | bytes 2097152

commit v3 on v2

--- a/solution.py
+++ b/solution.py
@@ -34,7 +34,7 @@
     return lax.dot_general(a, b, (dims, ((), ())), precision=lax.Precision.HIGHEST, preferred_element_type=F32)
 
 
-def inverses(grams):
+def inverses(grams, between=None):
     row = lax.broadcasted_iota(jnp.int32, (B, B), 0)
     col = lax.broadcasted_iota(jnp.int32, (B, B), 1)
     first = (col == row + 1) & ((row & 1) == 0)
@@ -52,23 +52,25 @@
         corner = ((row & -pair) == (col & -pair)) & ((row & width) == 0) & ((col & width) != 0)
         offs = [jnp.where(corner, gram, 0.0) for gram in grams]
         if width < 8:
-            inner = [dot6(inv, off) for inv, off in zip(invs, offs)]
-            invs = [inv - dot6(part, inv) for part, inv in zip(inner, invs)]
+            inner = [dot3(split(inv), split(off)) for inv, off in zip(invs, offs)]
+            invs = [inv - dot3(split(part), split(inv)) for part, inv in zip(inner, invs)]
         else:
             parts = [inv.reshape(B // pair, pair, B) for inv in invs]
             uppers = [part[:, :width].reshape(B // 2, B) for part in parts]
-            inner = [dot6(upper, off) for upper, off in zip(uppers, offs)]
-            uppers = [upper - dot6(part, inv) for upper, part, inv in zip(uppers, inner, invs)]
+            inner = [dot3(split(upper), split(off)) for upper, off in zip(uppers, offs)]
+            uppers = [upper - dot3(split(part), split(inv)) for upper, part, inv in zip(uppers, inner, invs)]
             invs = [
                 jnp.concatenate([upper.reshape(B // pair, width, B), part[:, width:]], axis=1).reshape(B, B)
                 for upper, part in zip(uppers, parts)
             ]
         width = pair
+        if between and width == 16:
+            between()
     return invs
 
 
-def reflectors(panels):
-    invs = inverses([dot6(panel, panel, ((0,), (0,))) for panel in panels])
+def reflectors(panels, between=None):
+    invs = inverses([dot6(panel, panel, ((0,), (0,))) for panel in panels], between)
     vs = [split(panel) for panel in panels]
     return [(v, dot3(v, split(inv))) for v, inv in zip(vs, invs)]
 
@@ -97,6 +99,8 @@
     mate, across = row_of(h, z, 1 - k), row_of(1 - h, z, k)
     prev_row, next_row = lax.rem(r + ROWS - 1, ROWS), lax.rem(r + 1, ROWS)
     other_col = lambda j: lax.rem(c + j + COLS, COLS)
+    in_line = lambda col, j: lax.div(col, 4) * 4 + lax.rem(col + j + 4, 4)
+    beside = lax.rem(c + 4, COLS)
     strip = lambda col: pl.ds(pl.multiple_of(col * PIECE, PIECE), PIECE)
     ids, sent = {}, []
 
@@ -133,8 +137,8 @@
             send(("ring", s, d), panels.at[s], gathered[s].at[k, z], ring_row(d), c)
         send(("mate", s, 0), panels.at[s], gathered[s].at[k, z], mate, c)
 
-    def receive(s, distances):
-        for d in distances:
+    def receive(s):
+        for d in (1, 7, 2, 6, 3, 5, 4):
             block = gathered[s].at[k, ring(-d)]
             arrive(("ring", s, d), block)
             send(("mate", s, d), block, block, mate, c)
@@ -143,8 +147,9 @@
         for d in range(RING):
             arrive(("mate", s, d), gathered[s].at[1 - k, ring(-d)])
 
-    near, distant = (1, 7, 2, 6), (3, 5, 4)
     ring_send(0)
+    ring_send(1)
+    ring_send(2)
     for s in range(SWEEPS):
         gathered[s][k, z] = panels[s]
 
@@ -157,14 +162,12 @@
 
     halves, places = zip(*[find(s, r - back) for s, back in WINDOWS])
     _, places_across = zip(*[find(s, across - back) for s, back in WINDOWS])
-    receive(0, near)
-    ring_send(1)
-    receive(0, distant)
+    receive(0)
+    ring_send(3)
     receive_mate(0)
     stage[0] = gathered[0][places[0]]
     far_out[0] = gathered[0][places_across[0]]
     wanted0[h, strip(c)] = gathered[0][places[0]]
-    ring_send(2)
     for flip, j in everyone:
         source = far_out if flip else stage
         send(("first share", flip, j), source.at[0], wanted0.at[h, strip(c)], across if flip else r, other_col(j))
@@ -187,27 +190,31 @@
             stage[w] = piece
             full[w - 1, strip(c)] = piece
         for w in ws:
-            for j in range(1, COLS):
-                send(("share", w, j), stage.at[w], full.at[w - 1, strip(c)], r, other_col(j))
-
-    receive(1, near)
-    ring_send(3)
-    receive(1, distant)
+            send(("beside", w), stage.at[w], full.at[w - 1, strip(c)], r, beside)
+        for w in ws:
+            for j in (1, 3, 2):
+                send(("share", w, j), stage.at[w], full.at[w - 1, strip(c)], r, in_line(c, j))
+
+    def relay(s):
+        for w in of_sweep[s]:
+            piece = full.at[w - 1, strip(beside)]
+            arrive(("beside", w), piece)
+            for j in (1, 3, 2):
+                send(("relay", w, j), piece, piece, r, in_line(c, j))
+
+    receive(1)
+    ring_send(4)
     cross(1)
-    receive(2, near)
-    ring_send(4)
-    receive(2, distant)
+    receive(2)
     cross(2)
-
     for flip, j in everyone:
         arrive(("first share", flip, j), wanted0.at[1 - h if flip else h, strip(other_col(-j))])
-    share(1)
-    (first,) = reflectors([wanted0[halves[0]]])
+    (first,) = reflectors([wanted0[halves[0]]], lambda: share(1))
+    share(2)
     hh[0, :B], hl[0, :B] = transform(first, True)
     hh[0, B:], hl[0, B:] = transform(first, False)
-    share(2)
-    receive(3, near + distant)
-    cross(3)
+    receive(3)
+    relay(1)
     z_copy.wait()
 
     def times(s, rows, block):
@@ -229,11 +236,14 @@
         new_high = times(s, high, split(mine[2 * B : 4 * B]))
         return times(s + 1, both, split(jnp.concatenate([new_low, new_high], axis=0)))
 
+    def await_shares(ws):
+        for w in ws:
+            for j in (1, 3, 2):
+                arrive(("share", w, j), full.at[w - 1, strip(in_line(c, -j))])
+                arrive(("relay", w, j), full.at[w - 1, strip(in_line(beside, -j))])
+
     def transforms(ws):
         s = WINDOWS[ws[0]][0]
-        for w in ws:
-            for j in range(1, COLS):
-                arrive(("share", w, j), full.at[w - 1, strip(other_col(-j))])
         own, back, even = reflectors([full[w - 1] for w in ws])
         hh[s, low], hl[s, low] = transform(back, False)
         hh[s, high], hl[s, high] = transform(own, True)
@@ -243,20 +253,29 @@
     for j in range(CHUNKS):
         cols = slice(j * CHUNK, (j + 1) * CHUNK)
         blocks[0, j, B : 3 * B] = times(0, both, split(z_in[:, cols]))
+        if j == 0:
+            relay(2)
+        if j == 1:
+            cross(3)
         if j:
             exchange(0, j - 1)
-    receive(4, near + distant)
+        if j == 2:
+            receive(4)
+    cross(4)
     exchange(0, CHUNKS - 1)
-    cross(4)
+    await_shares((1, 2, 3))
+    transforms((1, 2, 3))
     share(3)
-    transforms((1, 2, 3))
     share(4)
     for j in range(CHUNKS):
         blocks[1, j, B : 3 * B] = odd_even(0, j)
+        if j < 2:
+            relay(3 + j)
         if j:
             exchange(1, j - 1)
     z_in[0:8, 0:B] = jnp.zeros((8, B), F32)
     exchange(1, CHUNKS - 1)
+    await_shares((4, 5, 6))
     transforms((4, 5, 6))
     out_copies = []
     for j in range(CHUNKS):

time: 63.2 us -> 58.1 us (0.919)
  the two profiles are of different devices: /device:TPU:2 before, /device:TPU:1 now
where the time goes in v3:
time: 58.1 us; the launch traced here: 57.7 us
  Pallas kernels  55.3 us (95%)
  local copies, waits for them, and re-layouts  2.31 us (4%)
    pallas_call x1, Pallas kernels, on_device(): pl.pallas_call(kernel, out_shape=jax.ShapeDtypeStruct((rows, cols), F32),...  55.3 us
    unnamed x1, local copies, waits for them, and re-layouts  2.31 us

profile of v3, /device:TPU:1, one launch (start us, length us, event | category | flops | bytes accessed | tf_op | source)
XLA Modules:
  0.0 57.7 jit_solution(10524726301114934367)
XLA Ops:
  0.0 55.3 %shard_map.46 = f32[256,1024]{1,0:T(8,128)} custom-call(f32[256,1024]{1,0:T(8,128)} %z_hbm.1, f32[5,32,128]{2,1,0:T(8,128)} %bitcast.1, s32[5]{0:T(128)} %shift.1, s32[5,32]{1,0:T(8,128)} %slots.1), custom_call_target="tpu_custom_call" | custom-call | tf_op jit(solution)/shard_map/pallas_call | solution.py:295
  55.3 2.3 %copy.6 = f32[256,1024]{1,0:T(8,128)} copy(f32[256,1024]{1,0:T(8,128)} %shard_map.46) | data formatting | bytes 2097152

commit v4 on v2

--- a/solution.py
+++ b/solution.py
@@ -13,10 +13,9 @@
 RING = 8
 PIECE = 32
 WINDOWS = ((0, 0), (1, 0), (1, 1), (2, 0), (3, 0), (3, 1), (4, 0))
-LATER = len(WINDOWS) - 1
 CHUNK = 256
 CHUNKS = 1024 // CHUNK
-COPIES = 160
+COPIES = 130
 
 
 def split(a):
@@ -34,7 +33,7 @@
     return lax.dot_general(a, b, (dims, ((), ())), precision=lax.Precision.HIGHEST, preferred_element_type=F32)
 
 
-def inverses(grams):
+def inverses(grams, between=None):
     row = lax.broadcasted_iota(jnp.int32, (B, B), 0)
     col = lax.broadcasted_iota(jnp.int32, (B, B), 1)
     first = (col == row + 1) & ((row & 1) == 0)
@@ -52,23 +51,25 @@
         corner = ((row & -pair) == (col & -pair)) & ((row & width) == 0) & ((col & width) != 0)
         offs = [jnp.where(corner, gram, 0.0) for gram in grams]
         if width < 8:
-            inner = [dot6(inv, off) for inv, off in zip(invs, offs)]
-            invs = [inv - dot6(part, inv) for part, inv in zip(inner, invs)]
+            inner = [dot3(split(inv), split(off)) for inv, off in zip(invs, offs)]
+            invs = [inv - dot3(split(part), split(inv)) for part, inv in zip(inner, invs)]
         else:
             parts = [inv.reshape(B // pair, pair, B) for inv in invs]
             uppers = [part[:, :width].reshape(B // 2, B) for part in parts]
-            inner = [dot6(upper, off) for upper, off in zip(uppers, offs)]
-            uppers = [upper - dot6(part, inv) for upper, part, inv in zip(uppers, inner, invs)]
+            inner = [dot3(split(upper), split(off)) for upper, off in zip(uppers, offs)]
+            uppers = [upper - dot3(split(part), split(inv)) for upper, part, inv in zip(uppers, inner, invs)]
             invs = [
                 jnp.concatenate([upper.reshape(B // pair, width, B), part[:, width:]], axis=1).reshape(B, B)
                 for upper, part in zip(uppers, parts)
             ]
         width = pair
+        if between and width == 16:
+            between()
     return invs
 
 
-def reflectors(panels):
-    invs = inverses([dot6(panel, panel, ((0,), (0,))) for panel in panels])
+def reflectors(panels, between=None):
+    invs = inverses([dot6(panel, panel, ((0,), (0,))) for panel in panels], between)
     vs = [split(panel) for panel in panels]
     return [(v, dot3(v, split(inv))) for v, inv in zip(vs, invs)]
 
@@ -83,10 +84,10 @@
 
 def kernel(
     z_hbm, panels_hbm, shift, slots, out_hbm,
-    z_in, panels, gathered0, gathered1, gathered2, gathered3, gathered4, stage, wanted0,
-    far_out, far_in1, far_in2, far_in3, far_in4, full, blocks, outs, hh, hl, send_sem, recv_sem, own_sem,
+    z_in, panels, gathered0, gathered1, gathered2, gathered3, gathered4, near, far, along_x, pair, full,
+    blocks, outs, hh, hl, send_sem, recv_sem, own_sem,
 ):
-    gathered, far_in = (gathered0, gathered1, gathered2, gathered3, gathered4), (far_in1, far_in2, far_in3, far_in4)
+    gathered = gathered0, gathered1, gathered2, gathered3, gathered4
     r, c = lax.axis_index("row"), lax.axis_index("col")
     k = lax.rem(r, 2)
     z = lax.rem(lax.div(r, 2), RING)
@@ -96,8 +97,9 @@
     ring_row = lambda d: row_of(h, ring(d), k)
     mate, across = row_of(h, z, 1 - k), row_of(1 - h, z, k)
     prev_row, next_row = lax.rem(r + ROWS - 1, ROWS), lax.rem(r + 1, ROWS)
-    other_col = lambda j: lax.rem(c + j + COLS, COLS)
-    strip = lambda col: pl.ds(pl.multiple_of(col * PIECE, PIECE), PIECE)
+    x, y = lax.div(c, 4), lax.rem(c, 4)
+    in_line = lambda j: lax.rem(y + j + 4, 4)
+    beside = lax.rem(c + 4, COLS)
     ids, sent = {}, []
 
     def remote(name, src, dst, row, col):
@@ -117,8 +119,7 @@
 
     barrier = pltpu.get_barrier_semaphore()
     partners = [(ring_row(d), c) for d in range(1, RING)] + [(mate, c), (prev_row, c), (next_row, c)]
-    everyone = [(flip, j) for flip in (0, 1) for j in range(COLS) if (flip, j) != (0, 0)]
-    partners += [(across if flip else r, other_col(j)) for flip, j in everyone]
+    partners += [(r, beside), (across, c), (across, beside)] + [(r, x * 4 + in_line(j)) for j in (1, 2, 3)]
     for partner in partners:
         pl.semaphore_signal(barrier, inc=1, device_id=partner, device_id_type=MESH)
     panels_copy = pltpu.make_async_copy(panels_hbm, panels, own_sem.at[0])
@@ -128,8 +129,8 @@
     pl.semaphore_wait(barrier, len(partners))
     panels_copy.wait()
 
-    def ring_send(s):
-        for d in (4, 3, 5, 2, 6, 1, 7):
+    def ring_send(s, distances):
+        for d in distances:
             send(("ring", s, d), panels.at[s], gathered[s].at[k, z], ring_row(d), c)
         send(("mate", s, 0), panels.at[s], gathered[s].at[k, z], mate, c)
 
@@ -139,12 +140,22 @@
             arrive(("ring", s, d), block)
             send(("mate", s, d), block, block, mate, c)
 
+    def pass_on(s):
+        receive(s, (2, 6))
+        for d, origin, target in ((3, -2, 1), (5, 2, -1), (4, 4 * k - 2, 2 - 4 * k)):
+            block = gathered[s].at[k, ring(origin)]
+            send(("ring", s, d), block, block, ring_row(target), c)
+        receive(s, (1, 7))
+
+    straight, nearest, rest = (4, 3, 5, 2, 6, 1, 7), (2, 6, 1, 7), (3, 5, 4)
+
     def receive_mate(s):
         for d in range(RING):
             arrive(("mate", s, d), gathered[s].at[1 - k, ring(-d)])
 
-    near, distant = (1, 7, 2, 6), (3, 5, 4)
-    ring_send(0)
+    ring_send(0, straight)
+    ring_send(1, nearest)
+    ring_send(2, nearest)
     for s in range(SWEEPS):
         gathered[s][k, z] = panels[s]
 
@@ -157,57 +168,62 @@
 
     halves, places = zip(*[find(s, r - back) for s, back in WINDOWS])
     _, places_across = zip(*[find(s, across - back) for s, back in WINDOWS])
-    receive(0, near)
-    ring_send(1)
-    receive(0, distant)
-    receive_mate(0)
-    stage[0] = gathered[0][places[0]]
-    far_out[0] = gathered[0][places_across[0]]
-    wanted0[h, strip(c)] = gathered[0][places[0]]
-    ring_send(2)
-    for flip, j in everyone:
-        source = far_out if flip else stage
-        send(("first share", flip, j), source.at[0], wanted0.at[h, strip(c)], across if flip else r, other_col(j))
-
     of_sweep = [[w for w, (of, _) in enumerate(WINDOWS) if of == s] for s in range(SWEEPS)]
-
-    def cross(s):
+    span = [pl.ds(ws[0], len(ws)) for ws in of_sweep]
+
+    def spread(s):
         receive_mate(s)
-        ws = of_sweep[s]
-        for w in ws:
-            far_out[w] = gathered[s][places_across[w]]
-        span = pl.ds(ws[0], len(ws))
-        send(("far", s), far_out.at[span], far_in[s - 1].at[pl.ds(0, len(ws))], across, c)
+        for w in of_sweep[s]:
+            near[w] = gathered[s][places[w]]
+            far[w] = gathered[s][places_across[w]]
+        send(("near", s), near.at[span[s]], along_x.at[0, span[s]], r, beside)
+        send(("far", s), far.at[span[s]], along_x.at[1, span[s]], across, c)
+        send(("far beside", s), far.at[span[s]], along_x.at[2, span[s]], across, beside)
 
     def share(s):
-        ws = of_sweep[s]
-        arrive(("far", s), far_in[s - 1].at[pl.ds(0, len(ws))])
-        for i, w in enumerate(ws):
-            piece = jnp.where(halves[w] == h, gathered[s][places[w]], far_in[s - 1][i])
-            stage[w] = piece
-            full[w - 1, strip(c)] = piece
-        for w in ws:
-            for j in range(1, COLS):
-                send(("share", w, j), stage.at[w], full.at[w - 1, strip(c)], r, other_col(j))
-
-    receive(1, near)
-    ring_send(3)
-    receive(1, distant)
-    cross(1)
-    receive(2, near)
-    ring_send(4)
-    receive(2, distant)
-    cross(2)
-
-    for flip, j in everyone:
-        arrive(("first share", flip, j), wanted0.at[1 - h if flip else h, strip(other_col(-j))])
+        for i, name in enumerate(("near", "far", "far beside")):
+            arrive((name, s), along_x.at[i, span[s]])
+        for w in of_sweep[s]:
+            here = halves[w] == h
+            for of_x, piece in (
+                (x, jnp.where(here, near[w], along_x[1, w])),
+                (1 - x, jnp.where(here, along_x[0, w], along_x[2, w])),
+            ):
+                pair[w, of_x] = piece
+                full[w, of_x, y] = piece
+        for j in (1, 3, 2):
+            send(("share", s, j), pair.at[span[s]], full.at[span[s], :, y], r, x * 4 + in_line(j))
+
+    def await_share(s):
+        for j in (1, 3, 2):
+            arrive(("share", s, j), full.at[span[s], :, in_line(-j)])
+
+    receive(0, (1, 7, 2, 6, 3, 5, 4))
+    pass_on(1)
+    pass_on(2)
+    ring_send(3, nearest)
+    ring_send(4, nearest)
+    spread(0)
+    receive(1, rest)
+    spread(1)
+    share(0)
+    receive(2, rest)
+    spread(2)
+    pass_on(3)
+    pass_on(4)
     share(1)
-    (first,) = reflectors([wanted0[halves[0]]])
+    receive(3, rest)
+    receive(4, rest)
+    await_share(0)
+
+    def between():
+        share(2)
+        spread(3)
+        spread(4)
+
+    (first,) = reflectors([full[0].reshape(2 * B, B)], between)
     hh[0, :B], hl[0, :B] = transform(first, True)
     hh[0, B:], hl[0, B:] = transform(first, False)
-    share(2)
-    receive(3, near + distant)
-    cross(3)
     z_copy.wait()
 
     def times(s, rows, block):
@@ -231,10 +247,7 @@
 
     def transforms(ws):
         s = WINDOWS[ws[0]][0]
-        for w in ws:
-            for j in range(1, COLS):
-                arrive(("share", w, j), full.at[w - 1, strip(other_col(-j))])
-        own, back, even = reflectors([full[w - 1] for w in ws])
+        own, back, even = reflectors([full[w].reshape(2 * B, B) for w in ws])
         hh[s, low], hl[s, low] = transform(back, False)
         hh[s, high], hl[s, high] = transform(own, True)
         hh[s + 1, low], hl[s + 1, low] = transform(even, True)
@@ -245,18 +258,20 @@
         blocks[0, j, B : 3 * B] = times(0, both, split(z_in[:, cols]))
         if j:
             exchange(0, j - 1)
-    receive(4, near + distant)
+    await_share(1)
     exchange(0, CHUNKS - 1)
-    cross(4)
-    share(3)
+    await_share(2)
     transforms((1, 2, 3))
-    share(4)
     for j in range(CHUNKS):
         blocks[1, j, B : 3 * B] = odd_even(0, j)
         if j:
             exchange(1, j - 1)
+        if j in (1, 2):
+            share(j + 2)
     z_in[0:8, 0:B] = jnp.zeros((8, B), F32)
     exchange(1, CHUNKS - 1)
+    await_share(3)
+    await_share(4)
     transforms((4, 5, 6))
     out_copies = []
     for j in range(CHUNKS):
@@ -283,10 +298,10 @@
             pltpu.VMEM((SWEEPS, PIECE, B), F32),
             *[pltpu.VMEM((2, RING, PIECE, B), F32)] * SWEEPS,
             pltpu.VMEM((len(WINDOWS), PIECE, B), F32),
-            pltpu.VMEM((2, 2 * B, B), F32),
             pltpu.VMEM((len(WINDOWS), PIECE, B), F32),
-            *[pltpu.VMEM((2, PIECE, B), F32)] * (SWEEPS - 1),
-            pltpu.VMEM((LATER, 2 * B, B), F32),
+            pltpu.VMEM((3, len(WINDOWS), PIECE, B), F32),
+            pltpu.VMEM((len(WINDOWS), 2, PIECE, B), F32),
+            pltpu.VMEM((len(WINDOWS), 2, 4, PIECE, B), F32),
             pltpu.VMEM((2, CHUNKS, 4 * B, CHUNK), F32),
             pltpu.VMEM((CHUNKS, 2 * B, CHUNK), F32),
             pltpu.VMEM((SWEEPS, 2 * B, 2 * B), BF16),

time: 63.2 us -> 53.8 us (0.85)
  the two profiles are of different devices: /device:TPU:2 before, /device:TPU:1 now
where the time goes in v4:
time: 53.8 us; the launch traced here: 53.7 us
  Pallas kernels  51.3 us (95%)
  local copies, waits for them, and re-layouts  2.31 us (4%)
    pallas_call x1, Pallas kernels, on_device(): pl.pallas_call(kernel, out_shape=jax.ShapeDtypeStruct((rows, cols), F32),...  51.3 us
    unnamed x1, local copies, waits for them, and re-layouts  2.31 us

profile of v4, /device:TPU:1, one launch (start us, length us, event | category | flops | bytes accessed | tf_op | source)
XLA Modules:
  0.0 53.7 jit_solution(7968021159250906950)
XLA Ops:
  0.0 51.3 %shard_map.46 = f32[256,1024]{1,0:T(8,128)} custom-call(f32[256,1024]{1,0:T(8,128)} %z_hbm.1, f32[5,32,128]{2,1,0:T(8,128)} %bitcast.1, s32[5]{0:T(128)} %shift.1, s32[5,32]{1,0:T(8,128)} %slots.1), custom_call_target="tpu_custom_call" | custom-call | tf_op jit(solution)/shard_map/pallas_call | solution.py:291
  51.3 2.3 %copy.6 = f32[256,1024]{1,0:T(8,128)} copy(f32[256,1024]{1,0:T(8,128)} %shard_map.46) | data formatting | bytes 2097152

commit v5 on v4

--- a/solution.py
+++ b/solution.py
@@ -33,7 +33,7 @@
     return lax.dot_general(a, b, (dims, ((), ())), precision=lax.Precision.HIGHEST, preferred_element_type=F32)
 
 
-def inverses(grams, between=None):
+def inverses(grams, between):
     row = lax.broadcasted_iota(jnp.int32, (B, B), 0)
     col = lax.broadcasted_iota(jnp.int32, (B, B), 1)
     first = (col == row + 1) & ((row & 1) == 0)
@@ -63,12 +63,11 @@
                 for upper, part in zip(uppers, parts)
             ]
         width = pair
-        if between and width == 16:
-            between()
+        between.get(width, lambda: None)()
     return invs
 
 
-def reflectors(panels, between=None):
+def reflectors(panels, between):
     invs = inverses([dot6(panel, panel, ((0,), (0,))) for panel in panels], between)
     vs = [split(panel) for panel in panels]
     return [(v, dot3(v, split(inv))) for v, inv in zip(vs, invs)]
@@ -83,9 +82,9 @@
 
 
 def kernel(
-    z_hbm, panels_hbm, shift, slots, out_hbm,
+    z_hbm, panels_hbm, shift, slots, out_ref,
     z_in, panels, gathered0, gathered1, gathered2, gathered3, gathered4, near, far, along_x, pair, full,
-    blocks, outs, hh, hl, send_sem, recv_sem, own_sem,
+    blocks, hh, hl, send_sem, recv_sem, own_sem,
 ):
     gathered = gathered0, gathered1, gathered2, gathered3, gathered4
     r, c = lax.axis_index("row"), lax.axis_index("col")
@@ -168,22 +167,27 @@
 
     halves, places = zip(*[find(s, r - back) for s, back in WINDOWS])
     _, places_across = zip(*[find(s, across - back) for s, back in WINDOWS])
-    of_sweep = [[w for w, (of, _) in enumerate(WINDOWS) if of == s] for s in range(SWEEPS)]
-    span = [pl.ds(ws[0], len(ws)) for ws in of_sweep]
-
-    def spread(s):
-        receive_mate(s)
-        for w in of_sweep[s]:
+    def windows_of(*sweeps):
+        ws = [w for w, (of, _) in enumerate(WINDOWS) if of in sweeps]
+        return ws, pl.ds(ws[0], len(ws))
+
+    def spread(*sweeps):
+        ws, span = windows_of(*sweeps)
+        for s in sweeps:
+            receive_mate(s)
+        for w in ws:
+            s = WINDOWS[w][0]
             near[w] = gathered[s][places[w]]
             far[w] = gathered[s][places_across[w]]
-        send(("near", s), near.at[span[s]], along_x.at[0, span[s]], r, beside)
-        send(("far", s), far.at[span[s]], along_x.at[1, span[s]], across, c)
-        send(("far beside", s), far.at[span[s]], along_x.at[2, span[s]], across, beside)
-
-    def share(s):
+        send(("far", sweeps), far.at[span], along_x.at[1, span], across, c)
+        send(("far beside", sweeps), far.at[span], along_x.at[2, span], across, beside)
+        send(("near", sweeps), near.at[span], along_x.at[0, span], r, beside)
+
+    def share(*sweeps):
+        ws, span = windows_of(*sweeps)
         for i, name in enumerate(("near", "far", "far beside")):
-            arrive((name, s), along_x.at[i, span[s]])
-        for w in of_sweep[s]:
+            arrive((name, sweeps), along_x.at[i, span])
+        for w in ws:
             here = halves[w] == h
             for of_x, piece in (
                 (x, jnp.where(here, near[w], along_x[1, w])),
@@ -191,37 +195,38 @@
             ):
                 pair[w, of_x] = piece
                 full[w, of_x, y] = piece
+        for j in (2, 1, 3):
+            send(("share", sweeps, j), pair.at[span], full.at[span, :, y], r, x * 4 + in_line(j))
+
+    def await_share(*sweeps):
+        _, span = windows_of(*sweeps)
         for j in (1, 3, 2):
-            send(("share", s, j), pair.at[span[s]], full.at[span[s], :, y], r, x * 4 + in_line(j))
-
-    def await_share(s):
-        for j in (1, 3, 2):
-            arrive(("share", s, j), full.at[span[s], :, in_line(-j)])
-
-    receive(0, (1, 7, 2, 6, 3, 5, 4))
-    pass_on(1)
-    pass_on(2)
+            arrive(("share", sweeps, j), full.at[span, :, in_line(-j)])
+
+    receive(0, (1, 7, 2, 6))
     ring_send(3, nearest)
     ring_send(4, nearest)
+    pass_on(1)
+    receive(0, rest)
+    pass_on(2)
     spread(0)
     receive(1, rest)
+    pass_on(3)
+    pass_on(4)
     spread(1)
     share(0)
     receive(2, rest)
     spread(2)
-    pass_on(3)
-    pass_on(4)
     share(1)
     receive(3, rest)
     receive(4, rest)
     await_share(0)
 
-    def between():
+    def halfway():
         share(2)
-        spread(3)
-        spread(4)
-
-    (first,) = reflectors([full[0].reshape(2 * B, B)], between)
+        spread(3, 4)
+
+    (first,) = reflectors([full[0].reshape(2 * B, B)], {16: halfway})
     hh[0, :B], hl[0, :B] = transform(first, True)
     hh[0, B:], hl[0, B:] = transform(first, False)
     z_copy.wait()
@@ -245,9 +250,9 @@
         new_high = times(s, high, split(mine[2 * B : 4 * B]))
         return times(s + 1, both, split(jnp.concatenate([new_low, new_high], axis=0)))
 
-    def transforms(ws):
+    def transforms(ws, between={}):
         s = WINDOWS[ws[0]][0]
-        own, back, even = reflectors([full[w].reshape(2 * B, B) for w in ws])
+        own, back, even = reflectors([full[w].reshape(2 * B, B) for w in ws], between)
         hh[s, low], hl[s, low] = transform(back, False)
         hh[s, high], hl[s, high] = transform(own, True)
         hh[s + 1, low], hl[s + 1, low] = transform(even, True)
@@ -260,29 +265,21 @@
             exchange(0, j - 1)
     await_share(1)
     exchange(0, CHUNKS - 1)
+    share(3, 4)
     await_share(2)
     transforms((1, 2, 3))
     for j in range(CHUNKS):
         blocks[1, j, B : 3 * B] = odd_even(0, j)
         if j:
             exchange(1, j - 1)
-        if j in (1, 2):
-            share(j + 2)
     z_in[0:8, 0:B] = jnp.zeros((8, B), F32)
     exchange(1, CHUNKS - 1)
-    await_share(3)
-    await_share(4)
+    await_share(3, 4)
     transforms((4, 5, 6))
-    out_copies = []
     for j in range(CHUNKS):
-        outs[j] = odd_even(1, j)
-        cols = pl.ds(j * CHUNK, CHUNK)
-        out_copies.append(pltpu.make_async_copy(outs.at[j], out_hbm.at[:, cols], own_sem.at[2 + j]))
-        out_copies[-1].start()
+        out_ref[:, j * CHUNK : (j + 1) * CHUNK] = odd_even(1, j)
     for copy in sent:
         copy.wait_send()
-    for copy in out_copies:
-        copy.wait()
 
 
 def on_device(eigvecs, panels, sweep_shift, slot_group):
@@ -290,9 +287,9 @@
     hbm, smem = pl.BlockSpec(memory_space=pl.ANY), pl.BlockSpec(memory_space=pltpu.SMEM)
     return pl.pallas_call(
         kernel,
-        out_shape=jax.ShapeDtypeStruct((rows, cols), F32),
+        out_shape=pltpu.VMEM((rows, cols), F32),
         in_specs=[hbm, hbm, smem, smem],
-        out_specs=hbm,
+        out_specs=pl.BlockSpec(memory_space=pltpu.VMEM),
         scratch_shapes=[
             pltpu.VMEM((rows, cols), F32),
             pltpu.VMEM((SWEEPS, PIECE, B), F32),
@@ -303,12 +300,11 @@
             pltpu.VMEM((len(WINDOWS), 2, PIECE, B), F32),
             pltpu.VMEM((len(WINDOWS), 2, 4, PIECE, B), F32),
             pltpu.VMEM((2, CHUNKS, 4 * B, CHUNK), F32),
-            pltpu.VMEM((CHUNKS, 2 * B, CHUNK), F32),
             pltpu.VMEM((SWEEPS, 2 * B, 2 * B), BF16),
             pltpu.VMEM((SWEEPS, 2 * B, 2 * B), BF16),
             pltpu.SemaphoreType.DMA((COPIES,)),
             pltpu.SemaphoreType.DMA((COPIES,)),
-            pltpu.SemaphoreType.DMA((2 + CHUNKS,)),
+            pltpu.SemaphoreType.DMA((2,)),
         ],
         compiler_params=pltpu.CompilerParams(collective_id=0, has_side_effects=True),
     )(eigvecs, panels.reshape(SWEEPS, PIECE, B), sweep_shift, slot_group)

time: 53.8 us -> 54 us (level)
  Pallas kernels: 51.3 us -> 52.9 us
  local copies, waits for them, and re-layouts: 2.31 us -> 0.97 us
    pallas_call x1, Pallas kernels: 51.3 us -> 52.9 us  [on_device(): pl.pallas_call(kernel, out_shape=pltpu.VMEM((rows, cols), F32), in_specs=...]
    unnamed x1, local copies, waits for them, and re-layouts: 2.31 us -> 0.97 us
where the time goes in v5:
time: 54 us; the launch traced here: 53.9 us
  Pallas kernels  52.9 us (98%)
  local copies, waits for them, and re-layouts  0.97 us (2%)
    pallas_call x1, Pallas kernels, on_device(): pl.pallas_call(kernel, out_shape=pltpu.VMEM((rows, cols), F32), in_specs=...  52.9 us

profile of v5, /device:TPU:1, one launch (start us, length us, event | category | flops | bytes accessed | tf_op | source)
XLA Modules:
  0.0 53.9 jit_solution(15129946294018004884)
XLA Ops:
  0.0 52.9 %shard_map.46 = f32[256,1024]{1,0:T(8,128)S(1)} custom-call(f32[256,1024]{1,0:T(8,128)} %z_hbm.1, f32[5,32,128]{2,1,0:T(8,128)} %bitcast.1, s32[5]{0:T(128)} %shift.1, s32[5,32]{1,0:T(8,128)} %slots.1), custom_call_target="tpu_custom_call" | custom-call | tf_op jit(solution)/shard_map/pallas_call | solution.py:288
  52.9 1.0 %copy.6 = f32[256,1024]{1,0:T(8,128)} copy(f32[256,1024]{1,0:T(8,128)S(1)} %shard_map.46) | data formatting | bytes 2097152

commit v6 on v5

--- a/solution.py
+++ b/solution.py
@@ -23,14 +23,30 @@
     return high, (a - high.astype(F32)).astype(BF16)
 
 
+def split3(a):
+    high = a.astype(BF16)
+    rest = a - high.astype(F32)
+    middle = rest.astype(BF16)
+    return high, middle, (rest - middle.astype(F32)).astype(BF16)
+
+
+def dot_terms(a, b, terms, dims):
+    a = jnp.concatenate([a[i] for i, _ in terms], axis=dims[0][0])
+    b = jnp.concatenate([b[j] for _, j in terms], axis=dims[1][0])
+    return lax.dot_general(a, b, (dims, ((), ())), preferred_element_type=F32)
+
+
 def dot3(a, b, dims=((1,), (0,))):
-    (ah, al), (bh, bl) = a, b
-    dot = lambda x, y: lax.dot_general(x, y, (dims, ((), ())), preferred_element_type=F32)
-    return dot(ah, bh) + (dot(ah, bl) + dot(al, bh))
+    return dot_terms(a, b, ((1, 0), (0, 1), (0, 0)), dims)
 
 
 def dot6(a, b, dims=((1,), (0,))):
-    return lax.dot_general(a, b, (dims, ((), ())), precision=lax.Precision.HIGHEST, preferred_element_type=F32)
+    return dot_terms(a, b, ((2, 0), (0, 2), (1, 1), (1, 0), (0, 1), (0, 0)), dims)
+
+
+def gram_of(a):
+    dims = (((0,), (0,)), ((), ()))
+    return lax.dot_general(a, a, dims, precision=lax.Precision.HIGHEST, preferred_element_type=F32)
 
 
 def inverses(grams, between):
@@ -43,6 +59,13 @@
         down = 2.0 / jnp.sum(diagonal, axis=1, keepdims=True)
         along = 2.0 / jnp.sum(diagonal, axis=0, keepdims=True)
         return jnp.where(row == col, down, 0.0) - jnp.where(first, down * gram * along, 0.0)
+
+    def narrow(inv, off):
+        bands = [jnp.where((col - row == t) & ((col & (width - 1)) >= t), inv, 0.0) for t in range(width)]
+        inner = sum((pltpu.roll(off, t, 1) if t else off) * jnp.sum(band, axis=0, keepdims=True) for t, band in enumerate(bands))
+        return sum(
+            jnp.sum(band, axis=1, keepdims=True) * (pltpu.roll(inner, B - t, 0) if t else inner) for t, band in enumerate(bands)
+        )
 
     invs = [start(gram) for gram in grams]
     width = 2
@@ -50,14 +73,16 @@
         pair = 2 * width
         corner = ((row & -pair) == (col & -pair)) & ((row & width) == 0) & ((col & width) != 0)
         offs = [jnp.where(corner, gram, 0.0) for gram in grams]
-        if width < 8:
-            inner = [dot3(split(inv), split(off)) for inv, off in zip(invs, offs)]
-            invs = [inv - dot3(split(part), split(inv)) for part, inv in zip(inner, invs)]
+        if width < 8 and len(grams) == 1:
+            invs = [inv - narrow(inv, off) for inv, off in zip(invs, offs)]
+        elif width < 8:
+            inner = [dot6(split3(inv), split3(off)) for inv, off in zip(invs, offs)]
+            invs = [inv - dot6(split3(part), split3(inv)) for part, inv in zip(inner, invs)]
         else:
             parts = [inv.reshape(B // pair, pair, B) for inv in invs]
             uppers = [part[:, :width].reshape(B // 2, B) for part in parts]
-            inner = [dot3(split(upper), split(off)) for upper, off in zip(uppers, offs)]
-            uppers = [upper - dot3(split(part), split(inv)) for upper, part, inv in zip(uppers, inner, invs)]
+            inner = [dot6(split3(upper), split3(off)) for upper, off in zip(uppers, offs)]
+            uppers = [upper - dot6(split3(part), split3(inv)) for upper, part, inv in zip(uppers, inner, invs)]
             invs = [
                 jnp.concatenate([upper.reshape(B // pair, width, B), part[:, width:]], axis=1).reshape(B, B)
                 for upper, part in zip(uppers, parts)
@@ -68,9 +93,9 @@
 
 
 def reflectors(panels, between):
-    invs = inverses([dot6(panel, panel, ((0,), (0,))) for panel in panels], between)
+    invs = inverses([gram_of(panel) for panel in panels], between)
     vs = [split(panel) for panel in panels]
-    return [(v, dot3(v, split(inv))) for v, inv in zip(vs, invs)]
+    return [(v, dot6(split3(panel), split3(inv))) for v, panel, inv in zip(vs, panels, invs)]
 
 
 def transform(reflector, top):
@@ -206,10 +231,10 @@
     receive(0, (1, 7, 2, 6))
     ring_send(3, nearest)
     ring_send(4, nearest)
+    receive(0, rest)
     pass_on(1)
-    receive(0, rest)
+    spread(0)
     pass_on(2)
-    spread(0)
     receive(1, rest)
     pass_on(3)
     pass_on(4)
@@ -261,19 +286,14 @@
     for j in range(CHUNKS):
         cols = slice(j * CHUNK, (j + 1) * CHUNK)
         blocks[0, j, B : 3 * B] = times(0, both, split(z_in[:, cols]))
-        if j:
-            exchange(0, j - 1)
+        exchange(0, j)
     await_share(1)
-    exchange(0, CHUNKS - 1)
     share(3, 4)
     await_share(2)
     transforms((1, 2, 3))
     for j in range(CHUNKS):
         blocks[1, j, B : 3 * B] = odd_even(0, j)
-        if j:
-            exchange(1, j - 1)
-    z_in[0:8, 0:B] = jnp.zeros((8, B), F32)
-    exchange(1, CHUNKS - 1)
+        exchange(1, j)
     await_share(3, 4)
     transforms((4, 5, 6))
     for j in range(CHUNKS):

time: 54 us -> 56.9 us (1.054)
  the two profiles are of different devices: /device:TPU:1 before, /device:TPU:30 now
where the time goes in v6:
time: 56.9 us; the launch traced here: 56.8 us
  Pallas kernels  55.8 us (98%)
  local copies, waits for them, and re-layouts  0.97 us (2%)
    pallas_call x1, Pallas kernels, on_device(): pl.pallas_call(kernel, out_shape=pltpu.VMEM((rows, cols), F32), in_specs=...  55.8 us

profile of v6, /device:TPU:30, one launch (start us, length us, event | category | flops | bytes accessed | tf_op | source)
XLA Modules:
  0.0 56.8 jit_solution(2941285575061055383)
XLA Ops:
  0.0 55.8 %shard_map.46 = f32[256,1024]{1,0:T(8,128)S(1)} custom-call(f32[256,1024]{1,0:T(8,128)} %z_hbm.1, f32[5,32,128]{2,1,0:T(8,128)} %bitcast.1, s32[5]{0:T(128)} %shift.1, s32[5,32]{1,0:T(8,128)} %slots.1), custom_call_target="tpu_custom_call" | custom-call | tf_op jit(solution)/shard_map/pallas_call | solution.py:308
  55.8 1.0 %copy.6 = f32[256,1024]{1,0:T(8,128)} copy(f32[256,1024]{1,0:T(8,128)S(1)} %shard_map.46) | data formatting | bytes 2097152

commit v7 on v6

--- a/solution.py
+++ b/solution.py
@@ -246,12 +246,8 @@
     receive(3, rest)
     receive(4, rest)
     await_share(0)
-
-    def halfway():
-        share(2)
-        spread(3, 4)
-
-    (first,) = reflectors([full[0].reshape(2 * B, B)], {16: halfway})
+    spread(3, 4)
+    (first,) = reflectors([full[0].reshape(2 * B, B)], {16: lambda: share(2)})
     hh[0, :B], hl[0, :B] = transform(first, True)
     hh[0, B:], hl[0, B:] = transform(first, False)
     z_copy.wait()

time: 56.9 us -> 50.7 us (0.89)
  the two profiles are of different devices: /device:TPU:30 before, /device:TPU:1 now
where the time goes in v7:
time: 50.7 us; the launch traced here: 50.5 us
  Pallas kernels  49.6 us (98%)
  local copies, waits for them, and re-layouts  0.97 us (2%)
    pallas_call x1, Pallas kernels, on_device(): pl.pallas_call(kernel, out_shape=pltpu.VMEM((rows, cols), F32), in_specs=...  49.6 us

profile of v7, /device:TPU:1, one launch (start us, length us, event | category | flops | bytes accessed | tf_op | source)
XLA Modules:
  0.0 50.5 jit_solution(14261021002173265068)
XLA Ops:
  0.0 49.6 %shard_map.46 = f32[256,1024]{1,0:T(8,128)S(1)} custom-call(f32[256,1024]{1,0:T(8,128)} %z_hbm.1, f32[5,32,128]{2,1,0:T(8,128)} %bitcast.1, s32[5]{0:T(128)} %shift.1, s32[5,32]{1,0:T(8,128)} %slots.1), custom_call_target="tpu_custom_call" | custom-call | tf_op jit(solution)/shard_map/pallas_call | solution.py:304
  49.6 1.0 %copy.6 = f32[256,1024]{1,0:T(8,128)} copy(f32[256,1024]{1,0:T(8,128)S(1)} %shard_map.46) | data formatting | bytes 2097152

commit v8 on v7

--- a/solution.py
+++ b/solution.py
@@ -73,7 +73,7 @@
         pair = 2 * width
         corner = ((row & -pair) == (col & -pair)) & ((row & width) == 0) & ((col & width) != 0)
         offs = [jnp.where(corner, gram, 0.0) for gram in grams]
-        if width < 8 and len(grams) == 1:
+        if width == 2 or width < 8 and len(grams) == 1:
             invs = [inv - narrow(inv, off) for inv, off in zip(invs, offs)]
         elif width < 8:
             inner = [dot6(split3(inv), split3(off)) for inv, off in zip(invs, offs)]

time: 50.7 us -> 50.9 us (level)
  no operation moved by 1% of the time
where the time goes in v8:
time: 50.9 us; the launch traced here: 50.8 us
  Pallas kernels  49.8 us (98%)
  local copies, waits for them, and re-layouts  0.97 us (2%)
    pallas_call x1, Pallas kernels, on_device(): pl.pallas_call(kernel, out_shape=pltpu.VMEM((rows, cols), F32), in_specs=...  49.8 us

profile of v8, /device:TPU:1, one launch (start us, length us, event | category | flops | bytes accessed | tf_op | source)
XLA Modules:
  0.0 50.8 jit_solution(14607522266359310526)
XLA Ops:
  0.0 49.8 %shard_map.46 = f32[256,1024]{1,0:T(8,128)S(1)} custom-call(f32[256,1024]{1,0:T(8,128)} %z_hbm.1, f32[5,32,128]{2,1,0:T(8,128)} %bitcast.1, s32[5]{0:T(128)} %shift.1, s32[5,32]{1,0:T(8,128)} %slots.1), custom_call_target="tpu_custom_call" | custom-call | tf_op jit(solution)/shard_map/pallas_call | solution.py:304
  49.8 1.0 %copy.6 = f32[256,1024]{1,0:T(8,128)} copy(f32[256,1024]{1,0:T(8,128)S(1)} %shard_map.46) | data formatting | bytes 2097152
